TPU v7x, 256 devices: a whole 4x4x8 slice. The times are simulated.
256 devices in a mesh: scen: 64 (over y, z, core), link: 4 (over x).
Axes of the slice: x: 4, y: 4, z: 8, core: 2. Of those that a mesh axis runs over, the one named last changes fastest.
Arguments:
- factor_inv: bfloat16 [128, 1024, 1024], P('scen'), may hold values from -0.1875 to 0.1875
- coupling: bfloat16 [128, 1024, 1024], P('scen', None, 'link'), may hold values from -0.375 to 0.375
- first_diag: float32 [128, 128], P('scen'), may hold values from 1 to 10
- pattern: int32 [128, 8], P('scen'), may hold values from 0 to 127, as said below
Outputs:
- panel: float32 [16384, 128], P('scen')
- trailing: float32 [16384, 16384], P('scen', 'link')
Inputs may be any that keep to these rules, and one draw needn't show every extreme that they name: `pattern`: slot t of a scenario names a block of column range t // 2, that is, a block p with p // 32 = t // 2. The 2 scenarios of rows s * 2 to (s + 1) * 2 - 1 name every block at most once among them, and at most 1 block of any one group of blocks with the same p // 2. The first scenario of every such set names block 0 in slot 0.
All inputs are finite; a program needn't handle non-finite values.
Results may differ from a plain program's by a relative error of at most 0.0005.
Values may be sent and summed in bfloat16 or wider, within the bound.
No kernel may reach another device: no remote copies, remote signals or barrier semaphores. Data moves between devices by JAX's collectives and lax.ppermute only.
A program may use at most 128 MiB of HBM per device.

v0:
```python
import jax
import jax.numpy as jnp
from jax import lax
from jax.sharding import PartitionSpec as P


def broadcast(value, axis, source):
    kept = jnp.where(lax.axis_index(axis) == source, value, 0).astype(value.dtype)
    return lax.psum(kept, axis)


def per_device(factor_inv, coupling, first_diag, pattern):
    tile_size = first_diag.shape[1]
    rows_own = first_diag.shape[0]
    scen_count = lax.axis_size("scen")
    link_count = lax.axis_size("link")
    scen_pos = lax.axis_index("scen")
    link_pos = lax.axis_index("link")
    block_count = rows_own * scen_count
    per_link = block_count // link_count
    col_width = coupling.shape[2]
    slot_count = col_width // tile_size
    own_slabs = jnp.einsum(
        "snm,smc->snc", factor_inv, coupling, preferred_element_type=jnp.float32
    ).astype(jnp.bfloat16)
    contrib = jnp.einsum(
        "snr,snc->src",
        lax.all_gather(own_slabs, "link", axis=2, tiled=True),
        own_slabs,
        preferred_element_type=jnp.float32,
    )
    scen_here = contrib.shape[0]
    spread = pattern.shape[1]
    blocks = pattern.reshape(-1)
    tile_rows = contrib.reshape(scen_here * spread, tile_size, col_width)
    own_cols = (
        lax.dynamic_slice_in_dim(pattern, link_pos * slot_count, slot_count, 1)
        - link_pos * per_link
    )
    col_rows = jnp.broadcast_to(own_cols[:, None, :], (scen_here, spread, slot_count)).reshape(
        scen_here * spread, slot_count
    )
    col_range = jnp.arange(per_link, dtype=jnp.int32)
    outgoing = jnp.zeros((block_count, tile_size, col_width), jnp.float32).at[blocks].set(tile_rows)
    labels = jnp.full((block_count, slot_count), -1, jnp.int32).at[blocks].set(col_rows)
    arrived, arrived_cols = (
        lax.all_to_all(outgoing, "scen", split_axis=0, concat_axis=0, tiled=True),
        lax.all_to_all(labels, "scen", split_axis=0, concat_axis=0, tiled=True),
    )
    selector = (arrived_cols[:, :, None] == col_range[None, None, :]).astype(jnp.float32)
    selector = selector.reshape(scen_count, rows_own, slot_count, per_link)
    arrived = arrived.reshape(scen_count, rows_own, tile_size, slot_count, tile_size)
    summed = jnp.einsum("srkc,srxky->rxcy", selector, arrived, precision=lax.Precision.HIGHEST)
    global_rows = scen_pos * rows_own + jnp.arange(rows_own, dtype=jnp.int32)
    global_cols = link_pos * per_link + col_range
    on_diagonal = (global_rows[:, None] == global_cols[None, :]).astype(jnp.float32)
    unit_matrix = jnp.eye(tile_size, dtype=jnp.float32)
    diag_part = (
        on_diagonal[:, None, :, None]
        * (first_diag[:, :, None] * unit_matrix[None, :, :])[:, :, None, :]
    )
    schur = (summed + diag_part).reshape(rows_own * tile_size, per_link * tile_size)
    corner = broadcast(schur[:tile_size, :tile_size], "scen", 0)
    lead_factor = jnp.linalg.cholesky(corner)
    solved = jax.scipy.linalg.solve_triangular(lead_factor, schur[:, :tile_size].T, lower=True).T
    top_block = jnp.where(scen_pos == 0, lead_factor, solved[:tile_size])
    panel_mine = broadcast(jnp.concatenate([top_block, solved[tile_size:]], axis=0), "link", 0)
    gathered = lax.all_gather(panel_mine, "scen", axis=0, tiled=True)
    partner = lax.dynamic_slice_in_dim(
        gathered, link_pos * per_link * tile_size, per_link * tile_size, 0
    )
    trailing = schur - jnp.dot(
        panel_mine, partner.T, precision=lax.Precision.HIGHEST, preferred_element_type=jnp.float32
    )
    return (panel_mine, trailing)


def solution(mesh):
    in_specs = (P("scen", None, None), P("scen", None, "link"), P("scen", None), P("scen", None))
    out_specs = (P("scen", None), P("scen", "link"))
    return jax.shard_map(
        per_device, mesh=mesh, in_specs=in_specs, out_specs=out_specs, check_vma=False
    )
```

profile of v0, /device:TPU:1, one launch (start us, length us, event | category | flops | bytes accessed | tf_op | source)
XLA Modules:
  0.0 855.0 jit_solution(7507519871486025331)
XLA Ops:
  7.2 0.0 copy-start
  7.2 0.0 all-gather.3.cloned.1.call-start
  7.2 1.2 copy-done
  8.4 4.4 convolution_convert_fusion
  12.8 0.0 all-gather.3.cloned.1.call-update
  12.8 0.1 reshape.110
  12.9 0.1 dynamic-slice_subtract_fusion
  13.0 0.7 scatter_custom_fusion.1
  13.7 1.1 copy.30
  14.8 13.1 %all-to-all-start.1 = ((s32[64,2,2]{1,2,0:T(2,128)}), s32[64,2,2]{1,2,0:T(2,128)S(1)}, u32[]{:S(2)}, u32[]{:S(2)}) async-start(s32[64,2,2]{1,2,0:T(2,128)} %copy.30), calls=%async_computation.1 | async-start | bytes 131072 | tf_op jit(solution)/shard_map/all_to_all | solution.py:48
  27.9 41.4 %all-gather.3.cloned.1.call-done = bf16[2,1024,1024]{2,1,0:T(8,128)(2,1)} async-done(((bf16[2,1024,256]{2,1,0:T(8,128)(2,1)}), bf16[2,1024,1024]{2,1,0:T(8,128)(2,1)}) %all-gather.3.cloned.1.call-update) | async-done | bytes 4194320 | tf_op jit(solution)/shard_map/all_gather | solution.py:28
  69.3 4.2 fusion.15
  73.5 7.8 broadcast_in_dim.13
  81.4 3.7 scatter_fusion
  85.1 0.0 all-to-all-done.1
  85.1 12.4 %all-to-all-start = ((f32[128,128,256]{2,1,0:T(8,128)}), f32[128,128,256]{2,1,0:T(8,128)}, u32[]{:S(2)}, u32[]{:S(2)}) async-start(f32[128,128,256]{2,1,0:T(8,128)} %scatter_fusion), calls=%async_computation | async-start | bytes 33554432 | tf_op jit(solution)/shard_map/all_to_all | solution.py:47
  97.5 0.2 all-reduce.3.cloned.1.call-start
  97.8 0.1 compare_convert_fusion
  97.8 0.1 broadcast_multiply_fusion
  97.9 0.1 copy.31
  98.0 365.0 %all-to-all-done = f32[128,128,256]{2,1,0:T(8,128)} async-done(((f32[128,128,256]{2,1,0:T(8,128)}), f32[128,128,256]{2,1,0:T(8,128)}, u32[]{:S(2)}, u32[]{:S(2)}) %all-to-all-start) | async-done | bytes 16777248 | tf_op jit(solution)/shard_map/all_to_all | solution.py:47
  463.0 17.4 %copy.26 = f32[128,128,256]{1,2,0:T(8,128)} copy(f32[128,128,256]{2,1,0:T(8,128)} %all-to-all-done) | data formatting | bytes 33554432 | tf_op jit(solution)/shard_map/all_to_all | solution.py:47
  480.4 16.5 %copy.32 = f32[64,2,128,2,128]{4,0,3,2,1:T(8,128)} copy(f32[64,2,128,2,128]{2,4,3,1,0:T(8,128)} %bitcast.40) | data formatting | bytes 33554432 | tf_op jit(solution)/shard_map/reshape | solution.py:52
  496.9 9.5 %bitcast_add_fusion = f32[2,128,32,128]{3,2,1,0:T(8,128)S(1)} fusion(f32[64,2,128,2,128]{4,0,3,2,1:T(8,128)} %copy.32, f32[2,128,128]{2,1,0:T(8,128)S(1)} %broadcast_multiply_fusion, f32[2,32]{1,0:T(2,128)S(1)} %compare_convert_fusion, s32[64,2,2]{0,2,1:T(2,128)S(1)} %copy.31), kind=kOutput, calls=%fused_computation.4 | convolution fusion | flops 1612718080 | bytes 21103872 | tf_op jit(solution)/shard_map/srkc,srxky->rxcy/dot_general | solution.py:53
  506.5 3.9 copy.45
  510.4 0.0 copy-start.3
  510.4 2.0 copy-done.3
  512.4 0.6 slice_select_fusion.1
  513.0 0.0 all-reduce.3.cloned.1.call-update
  513.0 0.3 all-reduce.5.cloned.1.call-start
  513.3 167.0 %all-reduce.3.cloned.1.call-done = f32[128,128]{1,0:T(8,128)} async-done(((f32[128,128]{1,0:T(8,128)}), f32[128,128]{1,0:T(8,128)}) %all-reduce.3.cloned.1.call-update) | async-done | bytes 65552 | tf_op jit(solution)/shard_map/psum | solution.py:9
  680.3 0.9 copy.33
  681.2 0.9 fusion.4
  682.1 11.7 %cholesky.19 = f32[128,128]{1,0:T(8,128)S(1)} custom-call(f32[128,128]{1,0:T(8,128)S(1)} %fusion.4), custom_call_target="Cholesky" | custom-call | tf_op jit(solution)/shard_map/jit(cholesky)/cholesky | solution.py:64
  693.8 0.6 compare_reduce_fusion
  694.5 0.7 select_bitcast_fusion
  695.1 9.8 %custom-call.7 = f32[1,128,128]{1,2,0:T(8,128)S(1)} custom-call(f32[1,128,128]{2,1,0:T(8,128)S(1)} %select_bitcast_fusion), custom_call_target="InvertDiagBlocksLowerTriangular" | custom-call | tf_op jit(solution)/shard_map/jit(_solve_triangular)/triangular_solve | solution.py:65
  704.9 1.2 fusion.1
  706.1 0.7 slice_select_fusion
  706.8 0.7 maximum_select_fusion
  707.4 0.0 all-reduce.5.cloned.1.call-update
  707.5 0.3 all-gather.5.cloned.1.call-start
  707.8 41.0 %all-reduce.5.cloned.1.call-done = f32[256,128]{1,0:T(8,128)} async-done(((f32[256,128]{1,0:T(8,128)}), f32[256,128]{1,0:T(8,128)}) %all-reduce.5.cloned.1.call-update) | async-done | bytes 131088 | tf_op jit(solution)/shard_map/psum | solution.py:9
  748.7 0.0 all-gather.5.cloned.1.call-update
  748.8 0.0 copy-start.1
  748.8 88.6 %all-gather.5.cloned.1.call-done = f32[16384,128]{1,0:T(8,128)} async-done(((f32[256,128]{1,0:T(8,128)}), f32[16384,128]{1,0:T(8,128)}) %all-gather.5.cloned.1.call-update) | async-done | bytes 8388624 | tf_op jit(solution)/shard_map/all_gather | solution.py:68
  837.4 10.4 %convolution_subtract_fusion = f32[256,4096]{1,0:T(8,128)} fusion(f32[256,128]{1,0:T(8,128)} %all-reduce.5.cloned.1.call-done, f32[16384,128]{1,0:T(8,128)} %all-gather.5.cloned.1.call-done, s32[]{:T(128)S(6)} %select_n.51, f32[32,8,32,128]{3,2,1,0:T(8,128)} %bitcast.42), kind=kOutput, calls=%fused_computation.2 | convolution fusion | flops 1611661312 | bytes 10616836 | tf_op jit(solution)/shard_map/dot_general | solution.py:72
  847.8 0.7 copy.49
  (14 shorter events, 0.1 us)
Async XLA Ops:
  7.2 1.2 copy-start
  7.2 5.7 copy-start.6
  7.2 62.1 %all-gather.3.cloned.1.call-start = ((), (), s32[]{:S(2)}) async-start(), calls=%async_computation.2 | async-start | bytes 5242880 | tf_op jit(solution)/shard_map/all_gather | solution.py:28
  14.8 70.3 %all-to-all-start.1 = ((s32[64,2,2]{1,2,0:T(2,128)}), s32[64,2,2]{1,2,0:T(2,128)S(1)}, u32[]{:S(2)}, u32[]{:S(2)}) async-start(s32[64,2,2]{1,2,0:T(2,128)} %copy.30), calls=%async_computation.1 | async-start | bytes 131072 | tf_op jit(solution)/shard_map/all_to_all | solution.py:48
  85.1 12.8 %copy-start.5 = (f32[2,128]{1,0:T(2,128)S(1)}, f32[2,128]{1,0:T(2,128)}, u32[]{:S(2)}) copy-start(f32[2,128]{1,0:T(2,128)} %param.6) | copy-start | bytes 3076
  85.1 377.9 %all-to-all-start = ((f32[128,128,256]{2,1,0:T(8,128)}), f32[128,128,256]{2,1,0:T(8,128)}, u32[]{:S(2)}, u32[]{:S(2)}) async-start(f32[128,128,256]{2,1,0:T(8,128)} %scatter_fusion), calls=%async_computation | async-start | bytes 33554432 | tf_op jit(solution)/shard_map/all_to_all | solution.py:47
  97.5 582.8 %all-reduce.3.cloned.1.call-start = ((), (), s32[]{:S(2)}) async-start(), calls=%async_computation.3 | async-start | bytes 131072 | tf_op jit(solution)/shard_map/psum | solution.py:9
  506.4 3.9 copy-start.2
  510.4 2.0 copy-start.3
  513.0 235.7 %all-reduce.5.cloned.1.call-start = ((), (), s32[]{:S(2)}) async-start(), calls=%async_computation.4 | async-start | bytes 262144 | tf_op jit(solution)/shard_map/psum | solution.py:9
  707.5 129.9 %all-gather.5.cloned.1.call-start = ((), (), s32[]{:S(2)}) async-start(), calls=%async_computation.5 | async-start | bytes 8519680 | tf_op jit(solution)/shard_map/all_gather | solution.py:68
  748.8 99.7 %copy-start.1 = (bf16[2,1024,256]{2,1,0:T(8,128)(2,1)S(1)}, bf16[2,1024,256]{2,1,0:T(8,128)(2,1)}, u32[]{:S(2)}) copy-start(bf16[2,1024,256]{2,1,0:T(8,128)(2,1)} %param.5) | copy-start | bytes 3145732
  748.8 99.0 %copy-start.4 = (f32[256,128]{1,0:T(8,128)S(1)}, f32[256,128]{1,0:T(8,128)}, u32[]{:S(2)}) copy-start(f32[256,128]{1,0:T(8,128)} %all-reduce.5.cloned.1.call-done) | copy-start | bytes 393220
Sparse Core Ops, SparseCore 0:
  12.9 56.2 all-gather.2
  513.2 167.0 all-reduce.2
  707.6 41.0 all-reduce.4
  751.4 85.9 all-gather.4
where the time goes:
time: 856 us; the launch traced here: 855 us
  waiting for transfers between devices  703 us (82%)
  local copies, waits for them, and re-layouts  56.1 us (7%)
  matrix products  29.7 us (3%)
  starting transfers between devices  26.4 us (3%)
  other arithmetic  25.9 us (3%)
  between operations  14 us (2%)
    all_to_all x1, waiting for transfers between devices, per_device(): lax.all_to_all(outgoing, 'scen', split_axis=0, concat_axis=0, tiled=True)  365 us
    psum x2, waiting for transfers between devices, broadcast(): return lax.psum(kept, axis)  208 us
    all_gather x1, waiting for transfers between devices, per_device(): gathered = lax.all_gather(panel_mine, 'scen', axis=0, tiled=True)  88.6 us
    all_gather x1, waiting for transfers between devices, per_device(): lax.all_gather(own_slabs, 'link', axis=2, tiled=True)  41.4 us
    all_to_all x1, local copies, waits for them, and re-layouts, per_device(): lax.all_to_all(outgoing, 'scen', split_axis=0, concat_axis=0, tiled=True)  17.4 us
  transfers between devices with their start and end apart: 6, of which 5 were waited for; matrix products, arithmetic and copies ran while one was open for 2% of the time, Pallas kernels for 0%

commit v1 on v0

--- a/solution.py
+++ b/solution.py
@@ -65,7 +65,8 @@
     solved = jax.scipy.linalg.solve_triangular(lead_factor, schur[:, :tile_size].T, lower=True).T
     top_block = jnp.where(scen_pos == 0, lead_factor, solved[:tile_size])
     panel_mine = broadcast(jnp.concatenate([top_block, solved[tile_size:]], axis=0), "link", 0)
-    gathered = lax.all_gather(panel_mine, "scen", axis=0, tiled=True)
+    sent = jnp.stack([panel_mine] * lax.axis_size("scen"))
+    gathered = jnp.concatenate(lax.all_to_all(sent, "scen", 0, 0), axis=0)
     partner = lax.dynamic_slice_in_dim(
         gathered, link_pos * per_link * tile_size, per_link * tile_size, 0
     )

time: 856 us -> 971 us (1.13)
  waiting for transfers between devices: 703 us -> 800 us
  starting transfers between devices: 26.4 us -> 39.1 us
    all_to_all x0 -> x1, waiting for transfers between devices: none -> 186 us  [per_device(): gathered = jnp.concatenate(lax.all_to_all(sent, 'scen', 0, 0), axis=0)]
    all_gather x1 -> x0, waiting for transfers between devices: 88.6 us -> none  [per_device(): gathered = lax.all_gather(panel_mine, 'scen', axis=0, tiled=True)]
    all_to_all x0 -> x1, starting transfers between devices: none -> 13.1 us  [per_device(): gathered = jnp.concatenate(lax.all_to_all(sent, 'scen', 0, 0), axis=0)]
where the time goes in v1:
time: 971 us; the launch traced here: 970 us
  waiting for transfers between devices  800 us (82%)
  local copies, waits for them, and re-layouts  61.1 us (6%)
  starting transfers between devices  39.1 us (4%)
  matrix products  29.4 us (3%)
  other arithmetic  25.9 us (3%)
  between operations  13.9 us (1%)
    all_to_all x1, waiting for transfers between devices, per_device(): lax.all_to_all(outgoing, 'scen', split_axis=0, concat_axis=0, tiled=True)  365 us
    psum x2, waiting for transfers between devices, broadcast(): return lax.psum(kept, axis)  208 us
    all_to_all x1, waiting for transfers between devices, per_device(): gathered = jnp.concatenate(lax.all_to_all(sent, 'scen', 0, 0), axis=0)  186 us
    all_gather x1, waiting for transfers between devices, per_device(): lax.all_gather(own_slabs, 'link', axis=2, tiled=True)  41.4 us
  transfers between devices with their start and end apart: 6, of which 5 were waited for; matrix products, arithmetic and copies ran while one was open for 2% of the time, Pallas kernels for 0%

profile of v1, /device:TPU:1, one launch (start us, length us, event | category | flops | bytes accessed | tf_op | source)
XLA Modules:
  0.0 969.9 jit_solution(7598043602648062553)
XLA Ops:
  7.2 0.0 copy-start
  7.2 0.0 all-gather.2.cloned.1.call-start
  7.2 1.2 copy-done
  8.4 4.4 convolution_convert_fusion
  12.8 0.0 all-gather.2.cloned.1.call-update
  12.8 0.1 reshape.115
  12.9 0.1 dynamic-slice_subtract_fusion
  13.0 0.7 scatter_custom_fusion.1
  13.7 1.1 copy.30
  14.8 13.1 %all-to-all-start.1 = ((s32[64,2,2]{1,2,0:T(2,128)}), s32[64,2,2]{1,2,0:T(2,128)S(1)}, u32[]{:S(2)}, u32[]{:S(2)}) async-start(s32[64,2,2]{1,2,0:T(2,128)} %copy.30), calls=%async_computation.1 | async-start | bytes 131072 | tf_op jit(solution)/shard_map/all_to_all | solution.py:48
  27.9 41.4 %all-gather.2.cloned.1.call-done = bf16[2,1024,1024]{2,1,0:T(8,128)(2,1)} async-done(((bf16[2,1024,256]{2,1,0:T(8,128)(2,1)}), bf16[2,1024,1024]{2,1,0:T(8,128)(2,1)}) %all-gather.2.cloned.1.call-update) | async-done | bytes 4194320 | tf_op jit(solution)/shard_map/all_gather | solution.py:28
  69.3 4.2 fusion.15
  73.5 7.8 broadcast_in_dim.13
  81.4 3.7 scatter_fusion
  85.1 0.0 all-to-all-done.1
  85.1 12.4 %all-to-all-start = ((f32[128,128,256]{2,1,0:T(8,128)}), f32[128,128,256]{2,1,0:T(8,128)}, u32[]{:S(2)}, u32[]{:S(2)}) async-start(f32[128,128,256]{2,1,0:T(8,128)} %scatter_fusion), calls=%async_computation | async-start | bytes 33554432 | tf_op jit(solution)/shard_map/all_to_all | solution.py:47
  97.5 0.2 all-reduce.3.cloned.1.call-start
  97.7 0.1 compare_convert_fusion
  97.8 0.1 broadcast_multiply_fusion
  97.9 0.1 copy.31
  98.0 365.0 %all-to-all-done = f32[128,128,256]{2,1,0:T(8,128)} async-done(((f32[128,128,256]{2,1,0:T(8,128)}), f32[128,128,256]{2,1,0:T(8,128)}, u32[]{:S(2)}, u32[]{:S(2)}) %all-to-all-start) | async-done | bytes 16777248 | tf_op jit(solution)/shard_map/all_to_all | solution.py:47
  463.0 17.4 %copy.26 = f32[128,128,256]{1,2,0:T(8,128)} copy(f32[128,128,256]{2,1,0:T(8,128)} %all-to-all-done) | data formatting | bytes 33554432 | tf_op jit(solution)/shard_map/all_to_all | solution.py:47
  480.3 16.5 %copy.32 = f32[64,2,128,2,128]{4,0,3,2,1:T(8,128)} copy(f32[64,2,128,2,128]{2,4,3,1,0:T(8,128)} %bitcast.41) | data formatting | bytes 33554432 | tf_op jit(solution)/shard_map/reshape | solution.py:52
  496.8 9.5 bitcast_add_fusion
  506.3 0.0 copy-start.2
  506.4 3.9 copy.45
  510.2 0.0 copy-start.3
  510.3 2.0 copy-done.3
  512.3 0.6 slice_select_fusion.1
  512.9 0.0 all-reduce.3.cloned.1.call-update
  512.9 0.3 all-reduce.5.cloned.1.call-start
  513.2 167.0 %all-reduce.3.cloned.1.call-done = f32[128,128]{1,0:T(8,128)} async-done(((f32[128,128]{1,0:T(8,128)}), f32[128,128]{1,0:T(8,128)}) %all-reduce.3.cloned.1.call-update) | async-done | bytes 65552 | tf_op jit(solution)/shard_map/psum | solution.py:9
  680.2 0.9 copy.33
  681.1 0.9 fusion.4
  682.0 11.7 %cholesky.19 = f32[128,128]{1,0:T(8,128)S(1)} custom-call(f32[128,128]{1,0:T(8,128)S(1)} %fusion.4), custom_call_target="Cholesky" | custom-call | tf_op jit(solution)/shard_map/jit(cholesky)/cholesky | solution.py:64
  693.7 0.6 compare_reduce_fusion
  694.3 0.7 select_bitcast_fusion
  695.0 9.8 %custom-call.7 = f32[1,128,128]{1,2,0:T(8,128)S(1)} custom-call(f32[1,128,128]{2,1,0:T(8,128)S(1)} %select_bitcast_fusion), custom_call_target="InvertDiagBlocksLowerTriangular" | custom-call | tf_op jit(solution)/shard_map/jit(_solve_triangular)/triangular_solve | solution.py:65
  704.8 1.2 fusion.1
  706.0 0.7 slice_select_fusion
  706.7 0.7 maximum_select_fusion
  707.3 0.0 all-reduce.5.cloned.1.call-update
  707.4 41.3 %all-reduce.5.cloned.1.call-done = f32[256,128]{1,0:T(8,128)} async-done(((f32[256,128]{1,0:T(8,128)}), f32[256,128]{1,0:T(8,128)}) %all-reduce.5.cloned.1.call-update) | async-done | bytes 131088 | tf_op jit(solution)/shard_map/psum | solution.py:9
  748.6 5.1 stack.2
  753.8 13.1 %all-to-all-start.2 = ((f32[64,256,128]{2,1,0:T(8,128)}), f32[64,256,128]{2,1,0:T(8,128)}, u32[]{:S(2)}, u32[]{:S(2)}) async-start(f32[64,256,128]{2,1,0:T(8,128)} %stack.2), calls=%async_computation.2 | async-start | bytes 16777216 | tf_op jit(solution)/shard_map/all_to_all | solution.py:69
  766.8 185.7 %all-to-all-done.2 = f32[64,256,128]{2,1,0:T(8,128)} async-done(((f32[64,256,128]{2,1,0:T(8,128)}), f32[64,256,128]{2,1,0:T(8,128)}, u32[]{:S(2)}, u32[]{:S(2)}) %all-to-all-start.2) | async-done | bytes 8388640 | tf_op jit(solution)/shard_map/all_to_all | solution.py:69
  952.6 10.1 %convolution_subtract_fusion = f32[256,4096]{1,0:T(8,128)} fusion(f32[256,128]{1,0:T(8,128)S(1)} %copy-done.4, f32[16384,128]{1,0:T(8,128)} %bitcast.13, s32[]{:T(128)S(6)} %select_n.51, f32[32,8,32,128]{3,2,1,0:T(8,128)} %bitcast.43), kind=kOutput, calls=%fused_computation.2 | convolution fusion | flops 1611661312 | bytes 10616836 | tf_op jit(solution)/shard_map/dot_general | solution.py:73
  962.7 0.7 copy.49
  (14 shorter events, 0.1 us)
Async XLA Ops:
  7.2 1.2 copy-start
  7.2 5.7 copy-start.6
  7.2 62.1 %all-gather.2.cloned.1.call-start = ((), (), s32[]{:S(2)}) async-start(), calls=%async_computation.3 | async-start | bytes 5242880 | tf_op jit(solution)/shard_map/all_gather | solution.py:28
  14.8 70.3 %all-to-all-start.1 = ((s32[64,2,2]{1,2,0:T(2,128)}), s32[64,2,2]{1,2,0:T(2,128)S(1)}, u32[]{:S(2)}, u32[]{:S(2)}) async-start(s32[64,2,2]{1,2,0:T(2,128)} %copy.30), calls=%async_computation.1 | async-start | bytes 131072 | tf_op jit(solution)/shard_map/all_to_all | solution.py:48
  85.1 12.8 %copy-start.5 = (f32[2,128]{1,0:T(2,128)S(1)}, f32[2,128]{1,0:T(2,128)}, u32[]{:S(2)}) copy-start(f32[2,128]{1,0:T(2,128)} %param.6) | copy-start | bytes 3076
  85.1 377.9 %all-to-all-start = ((f32[128,128,256]{2,1,0:T(8,128)}), f32[128,128,256]{2,1,0:T(8,128)}, u32[]{:S(2)}, u32[]{:S(2)}) async-start(f32[128,128,256]{2,1,0:T(8,128)} %scatter_fusion), calls=%async_computation | async-start | bytes 33554432 | tf_op jit(solution)/shard_map/all_to_all | solution.py:47
  97.5 582.7 %all-reduce.3.cloned.1.call-start = ((), (), s32[]{:S(2)}) async-start(), calls=%async_computation.4 | async-start | bytes 131072 | tf_op jit(solution)/shard_map/psum | solution.py:9
  506.3 3.9 copy-start.2
  510.2 2.0 copy-start.3
  512.9 235.7 %all-reduce.5.cloned.1.call-start = ((), (), s32[]{:S(2)}) async-start(), calls=%async_computation.5 | async-start | bytes 262144 | tf_op jit(solution)/shard_map/psum | solution.py:9
  753.8 198.8 %copy-start.4 = (f32[256,128]{1,0:T(8,128)S(1)}, f32[256,128]{1,0:T(8,128)}, u32[]{:S(2)}) copy-start(f32[256,128]{1,0:T(8,128)} %all-reduce.5.cloned.1.call-done) | copy-start | bytes 393220
  753.8 198.8 %all-to-all-start.2 = ((f32[64,256,128]{2,1,0:T(8,128)}), f32[64,256,128]{2,1,0:T(8,128)}, u32[]{:S(2)}, u32[]{:S(2)}) async-start(f32[64,256,128]{2,1,0:T(8,128)} %stack.2), calls=%async_computation.2 | async-start | bytes 16777216 | tf_op jit(solution)/shard_map/all_to_all | solution.py:69
  952.6 10.8 %copy-start.1 = (bf16[2,1024,256]{2,1,0:T(8,128)(2,1)S(1)}, bf16[2,1024,256]{2,1,0:T(8,128)(2,1)}, u32[]{:S(2)}) copy-start(bf16[2,1024,256]{2,1,0:T(8,128)(2,1)} %param.5) | copy-start | bytes 3145732
Sparse Core Ops, SparseCore 0:
  12.9 56.2 all-gather.1
  513.0 167.0 all-reduce.2
  707.5 41.0 all-reduce.4
